TPU v7x, 32 devices: a whole 2x2x4 slice. The times are simulated.
32 devices in a mesh: expert: 16 (over z, x, core), tensor: 2 (over y).
Axes of the slice: x: 2, y: 2, z: 4, core: 2. Of those that a mesh axis runs over, the one named last changes fastest.
Arguments:
- tokens: bfloat16 [256, 7168], P('expert', 'tensor'), may hold values from -6 to 6
- expert_ids: int32 [256, 8], P('expert'), may hold values from 0 to 7, as said below
- route_weights: float32 [256, 8], P('expert'), may hold values from 0.05 to 1
- gate_weight: bfloat16 [16, 512, 7168], P('expert', 'tensor'), may hold values from -0.0625 to 0.0625
- up_weight: bfloat16 [16, 512, 7168], P('expert', 'tensor'), may hold values from -0.0625 to 0.0625
- down_weight: bfloat16 [16, 512, 7168], P('expert', 'tensor'), may hold values from -0.1875 to 0.1875
Outputs:
- mixed: bfloat16 [256, 7168], P('expert', 'tensor')
Inputs may be any that keep to these rules, and one draw needn't show every extreme that they name: `expert_ids`: each row holds 8 different experts. One expert, the same for all tokens, is named by exactly 16 of the 16 tokens of every block of 16 consecutive tokens; every other expert by at most 16 tokens of a block.
All inputs are finite; a program needn't handle non-finite values.
Results may differ from a plain program's by a relative error of at most 0.015.
Values may be sent and summed in bfloat16 or wider, within the bound.
A program may use at most 64 MiB of HBM per device.

v0:
```python
import jax
import jax.numpy as jnp
from jax import lax
from jax.sharding import PartitionSpec as P


def rows_times(rows, weight):
    return lax.dot_general(
        rows, weight, (((1,), (1,)), ((), ())), preferred_element_type=jnp.float32
    )


def body(tokens, expert_ids, route_weights, gate_weight, up_weight, down_weight):
    devices_wide = lax.axis_size("expert")
    experts = devices_wide // 2
    tok_count = expert_ids.shape[0]
    per_token = expert_ids.shape[1]
    capacity = min(tok_count, tok_count * per_token // experts)
    slot_count = experts * capacity
    arrived_count = devices_wide * capacity
    expert_range = jnp.arange(experts, dtype=jnp.int32)
    onehot = jnp.sum(
        (expert_ids[:, :, None] == expert_range[None, None, :]).astype(jnp.int32), axis=1
    )
    earlier_count = jnp.cumsum(onehot, axis=0) - onehot
    slot_rank = jnp.take_along_axis(earlier_count, expert_ids, axis=1)
    slot_of = expert_ids * capacity + slot_rank
    slot_range = jnp.arange(slot_count, dtype=jnp.int32)
    select = jnp.any(slot_of[None, :, :] == slot_range[:, None, None], axis=2).astype(jnp.bfloat16)
    weight_gate = gate_weight[0]
    weight_up = up_weight[0]
    weight_out = down_weight[0]
    whole_rows = lax.all_gather(tokens, "tensor", axis=1, tiled=True)
    packed = jnp.dot(select, whole_rows, preferred_element_type=jnp.float32).astype(jnp.bfloat16)
    packed = packed.reshape(experts, capacity, whole_rows.shape[1])
    arrived = lax.all_to_all(
        jnp.repeat(packed, 2, axis=0), "expert", split_axis=0, concat_axis=0, tiled=True
    ).reshape(arrived_count, -1)
    gate_act = rows_times(arrived, weight_gate)
    up_act = rows_times(arrived, weight_up)
    hidden = (jax.nn.silu(gate_act) * up_act).astype(jnp.bfloat16)
    columns = lax.all_to_all(weight_out, "tensor", split_axis=1, concat_axis=0, tiled=True)
    unit_count = hidden.shape[1]
    shard_piece = lax.all_gather(hidden, "tensor", axis=1, tiled=True)
    groups = shard_piece.shape[1] // unit_count
    weight_rows = columns
    weight_rows = weight_rows.reshape(groups, unit_count, columns.shape[1])
    grouped = shard_piece.reshape(shard_piece.shape[0], groups, unit_count)
    group_terms = jnp.einsum(
        "rgf,gfd->grd", grouped, weight_rows, preferred_element_type=jnp.float32
    ).astype(jnp.bfloat16)
    group_terms = lax.optimization_barrier(group_terms)
    half_out = jnp.sum(group_terms.astype(jnp.float32), axis=0).astype(jnp.bfloat16)
    returned = lax.all_to_all(
        half_out.reshape(devices_wide, capacity, -1),
        "expert",
        split_axis=0,
        concat_axis=0,
        tiled=True,
    )
    returned = returned.reshape(experts, 2, capacity, -1).astype(jnp.float32)
    combined = (returned[:, 0] + returned[:, 1]).reshape(slot_count, -1)
    picked = combined[slot_of]
    mixed_out = jnp.sum(route_weights[:, :, None] * picked, axis=1)
    return mixed_out.astype(jnp.bfloat16)


def solution(mesh):
    placed = (
        P("expert", "tensor"),
        P("expert", None),
        P("expert", None),
        P("expert", "tensor", None),
        P("expert", "tensor", None),
        P("expert", "tensor", None),
    )
    return jax.shard_map(
        body, mesh=mesh, in_specs=placed, out_specs=P("expert", "tensor"), check_vma=False
    )
```

profile of v0, /device:TPU:11, one launch (start us, length us, event | category | flops | bytes accessed | tf_op | source)
XLA Modules:
  0.0 212.2 jit_solution(18340728612617636076)
XLA Ops:
  0.0 0.7 convert_reduce_fusion
  0.7 0.7 bitcast_or_fusion
  1.4 0.1 copy.24
  1.5 0.1 copy.26
  1.6 0.1 reshape.55
  1.7 0.0 copy-start.1
  1.7 0.0 copy-start
  1.7 1.3 gather_fusion.1
  3.0 0.1 reshape.58
  3.1 0.1 copy.27
  3.1 0.0 copy-done.1
  3.2 0.1 copy.28
  3.2 0.1 fusion.14
  3.3 0.0 copy-done
  3.3 4.7 %all_gather.6 = bf16[16,7168]{1,0:T(8,128)(2,1)S(1)} all-gather(bf16[16,3584]{1,0:T(8,128)(2,1)S(1)} %copy-done), channel_id=1, replica_groups=mesh['expert'=16,'tensor'=2] {'tensor'}, dimensions={1}, use_global_device_ids=true | all-gather | bytes 344064 | tf_op jit(solution)/shard_map/all_gather | solution.py:33
  8.0 0.7 convolution_convert_fusion
  8.7 2.3 %broadcast_in_dim.16 = bf16[8,2,16,7168]{3,2,1,0:T(8,128)(2,1)} broadcast(bf16[8,16,7168]{2,1,0:T(8,128)(2,1)S(1)} %bitcast.41), dimensions={0,2,3} | broadcast | bytes 5505024 | tf_op jit(solution)/shard_map/broadcast_in_dim | solution.py:37
  11.1 7.4 %all-to-all-start = ((bf16[16,16,7168]{2,1,0:T(8,128)(2,1)}), bf16[16,16,7168]{2,1,0:T(8,128)(2,1)}, u32[]{:S(2)}, u32[]{:S(2)}) async-start(bf16[16,16,7168]{2,1,0:T(8,128)(2,1)} %bitcast.39), calls=%async_computation | async-start | bytes 7340032 | tf_op jit(solution)/shard_map/all_to_all | solution.py:36
  18.4 5.9 %copy.29 = bf16[1,256,7168]{1,2,0:T(8,128)(2,1)} copy(bf16[1,256,7168]{2,1,0:T(8,128)(2,1)} %param.11) | data formatting | bytes 7340032 | tf_op args[5]
  24.4 6.0 %copy.30 = bf16[256,2,3584]{2,0,1:T(8,128)(2,1)} copy(bf16[256,2,3584]{0,2,1:T(8,128)(2,1)} %bitcast.38) | data formatting | bytes 7340032 | tf_op jit(solution)/shard_map/all_to_all | solution.py:42
  30.3 69.4 %all-to-all-done = bf16[16,16,7168]{2,1,0:T(8,128)(2,1)} async-done(((bf16[16,16,7168]{2,1,0:T(8,128)(2,1)}), bf16[16,16,7168]{2,1,0:T(8,128)(2,1)}, u32[]{:S(2)}, u32[]{:S(2)}) %all-to-all-start) | async-done | bytes 3670048 | tf_op jit(solution)/shard_map/all_to_all | solution.py:36
  99.7 5.5 %all-to-all-start.1 = ((bf16[256,2,3584]{2,0,1:T(8,128)(2,1)}), bf16[256,2,3584]{2,0,1:T(8,128)(2,1)}, u32[]{:S(2)}, u32[]{:S(2)}) async-start(bf16[256,2,3584]{2,0,1:T(8,128)(2,1)} %copy.30), calls=%async_computation.1 | async-start | bytes 7340032 | tf_op jit(solution)/shard_map/all_to_all | solution.py:42
  105.2 0.0 copy-start.3
  105.2 4.4 %fusion.3 = f32[256,256]{1,0:T(8,128)S(1)} fusion(bf16[256,7168]{1,0:T(8,128)(2,1)} %bitcast.3, bf16[1,256,7168]{2,1,0:T(8,128)(2,1)} %param.9), kind=kOutput, calls=%fused_computation.7 | convolution fusion | flops 939524096 | bytes 7602176 | tf_op jit(solution)/shard_map/dot_general | solution.py:8
  109.6 0.0 copy-done.3
  109.6 3.2 %fusion.9 = bf16[256,256]{1,0:T(8,128)(2,1)S(1)} fusion(bf16[256,7168]{1,0:T(8,128)(2,1)} %bitcast.3, bf16[1,256,7168]{2,1,0:T(8,128)(2,1)S(1)} %copy-done.3, f32[256,256]{1,0:T(8,128)S(1)} %fusion.3), kind=kOutput, calls=%fused_computation.13 | convolution fusion | flops 939917312 | bytes 7733248 | tf_op jit(solution)/shard_map/dot_general | solution.py:8
  112.8 36.8 %all_gather.7 = bf16[256,512]{1,0:T(8,128)(2,1)S(1)} all-gather(bf16[256,256]{1,0:T(8,128)(2,1)S(1)} %fusion.9), channel_id=1, replica_groups=mesh['expert'=16,'tensor'=2] {'tensor'}, dimensions={1}, use_global_device_ids=true | all-gather | bytes 393216 | tf_op jit(solution)/shard_map/all_gather | solution.py:44
  149.6 0.0 all-to-all-done.1
  149.6 5.0 %convolution_convert_fusion.1 = bf16[2,256,3584]{2,1,0:T(8,128)(2,1)} fusion(bf16[256,2,3584]{2,0,1:T(8,128)(2,1)} %all-to-all-done.1, bf16[32,2,8,256]{3,2,1,0:T(8,128)(2,1)S(1)} %bitcast.42), kind=kOutput, calls=%fused_computation.3 | convolution fusion | flops 941359104 | bytes 7602176 | tf_op jit(solution)/shard_map/rgf,gfd->grd/dot_general | solution.py:49
  154.6 0.0 copy-start.2
  154.6 4.4 %reduce_sum.31 = bf16[256,3584]{1,0:T(8,128)(2,1)} reduce(bf16[2,256,3584]{2,1,0:T(8,128)(2,1)} %convolution_convert_fusion.1, bf16[]{:T(256)} %constant.31.clone.1), dimensions={0}, to_apply=%region_3.4 | reduce | flops 917504 | bytes 5505026 | tf_op jit(solution)/shard_map/reduce_sum | solution.py:53
  159.0 5.6 %all-to-all-start.2 = ((bf16[16,16,3584]{2,1,0:T(8,128)(2,1)}), bf16[16,16,3584]{2,1,0:T(8,128)(2,1)S(1)}, u32[]{:S(2)}, u32[]{:S(2)}) async-start(bf16[16,16,3584]{2,1,0:T(8,128)(2,1)} %bitcast.8), calls=%async_computation.2 | async-start | bytes 3670016 | tf_op jit(solution)/shard_map/all_to_all | solution.py:54
  164.6 0.1 copy.32
  164.7 0.1 reshape.49
  164.8 0.0 copy-done.2
  164.8 0.1 copy.23
  164.9 41.6 %all-to-all-done.2 = bf16[16,16,3584]{2,1,0:T(8,128)(2,1)S(1)} async-done(((bf16[16,16,3584]{2,1,0:T(8,128)(2,1)}), bf16[16,16,3584]{2,1,0:T(8,128)(2,1)S(1)}, u32[]{:S(2)}, u32[]{:S(2)}) %all-to-all-start.2) | async-done | bytes 1835040 | tf_op jit(solution)/shard_map/all_to_all | solution.py:54
  206.4 0.4 convert.2
  206.9 0.2 slice_add_fusion
  207.1 2.4 %gather_fusion = f32[128,3584]{1,0:T(8,128)} fusion(f32[128,3584]{1,0:T(8,128)S(1)} %bitcast.37, s32[1024]{0:T(1024)S(1)} %pad_clamp_fusion), kind=kCustom, calls=%fused_computation | custom fusion | bytes 3670528 | tf_op jit(solution)/shard_map/gather | solution.py:63
  209.5 2.8 %fusion.5 = bf16[16,3584]{1,0:T(8,128)(2,1)} fusion(f32[128,3584]{1,0:T(8,128)} %gather_fusion, f32[16,8]{1,0:T(8,128)S(1)} %copy.23), kind=kLoop, calls=%fused_computation.11 | loop fusion | flops 860160 | bytes 1950208 | tf_op jit(solution)/shard_map/reduce_sum | solution.py:64
  (4 shorter events, 0.1 us)
Async XLA Ops:
  1.7 1.5 copy-start.1
  1.7 1.6 copy-start
  11.1 88.6 %all-to-all-start = ((bf16[16,16,7168]{2,1,0:T(8,128)(2,1)}), bf16[16,16,7168]{2,1,0:T(8,128)(2,1)}, u32[]{:S(2)}, u32[]{:S(2)}) async-start(bf16[16,16,7168]{2,1,0:T(8,128)(2,1)} %bitcast.39), calls=%async_computation | async-start | bytes 7340032 | tf_op jit(solution)/shard_map/all_to_all | solution.py:36
  99.7 49.9 %all-to-all-start.1 = ((bf16[256,2,3584]{2,0,1:T(8,128)(2,1)}), bf16[256,2,3584]{2,0,1:T(8,128)(2,1)}, u32[]{:S(2)}, u32[]{:S(2)}) async-start(bf16[256,2,3584]{2,0,1:T(8,128)(2,1)} %copy.30), calls=%async_computation.1 | async-start | bytes 7340032 | tf_op jit(solution)/shard_map/all_to_all | solution.py:42
  105.2 4.5 %copy-start.3 = (bf16[1,256,7168]{2,1,0:T(8,128)(2,1)S(1)}, bf16[1,256,7168]{2,1,0:T(8,128)(2,1)}, u32[]{:S(2)}) copy-start(bf16[1,256,7168]{2,1,0:T(8,128)(2,1)} %param.10) | copy-start | bytes 11010052
  154.6 10.2 %copy-start.2 = (f32[16,8]{0,1:T(8,128)S(1)}, f32[16,8]{0,1:T(8,128)}, u32[]{:S(2)}) copy-start(f32[16,8]{0,1:T(8,128)} %param.8) | copy-start | bytes 1540
  159.0 47.4 %all-to-all-start.2 = ((bf16[16,16,3584]{2,1,0:T(8,128)(2,1)}), bf16[16,16,3584]{2,1,0:T(8,128)(2,1)S(1)}, u32[]{:S(2)}, u32[]{:S(2)}) async-start(bf16[16,16,3584]{2,1,0:T(8,128)(2,1)} %bitcast.8), calls=%async_computation.2 | async-start | bytes 3670016 | tf_op jit(solution)/shard_map/all_to_all | solution.py:54
where the time goes:
time: 213 us; the launch traced here: 212 us
  waiting for transfers between devices  111 us (52%)
  blocking collectives  41.5 us (19%)
  local copies, waits for them, and re-layouts  18.6 us (9%)
  starting transfers between devices  18.5 us (9%)
  matrix products  13.3 us (6%)
  other arithmetic  9.36 us (4%)
    all_to_all x1, waiting for transfers between devices, body(): lax.all_to_all(jnp.repeat(packed, 2, axis=0), 'expert', split_axis=0, con...  69.4 us
    all_to_all x1, waiting for transfers between devices, body(): lax.all_to_all(half_out.reshape(devices_wide, capacity, -1), 'expert', sp...  41.6 us
    all_gather x1, blocking collectives, body(): shard_piece = lax.all_gather(hidden, 'tensor', axis=1, tiled=True)  36.8 us
    dot_general x2, matrix products, rows_times(): lax.dot_general(rows, weight, (((1,), (1,)), ((), ())), preferred_element...  7.63 us
    all_to_all x1, starting transfers between devices, body(): lax.all_to_all(jnp.repeat(packed, 2, axis=0), 'expert', split_axis=0, con...  7.38 us
    unnamed x10, local copies, waits for them, and re-layouts  6.01 us
    all_to_all x1, local copies, waits for them, and re-layouts, body(): lax.all_to_all(weight_out, 'tensor', split_axis=1, concat_axis=0, tiled=T...  5.95 us
    all_to_all x1, starting transfers between devices, body(): lax.all_to_all(half_out.reshape(devices_wide, capacity, -1), 'expert', sp...  5.63 us
  transfers between devices with their start and end apart: 3, of which 2 were waited for; matrix products, arithmetic and copies ran while one was open for 9% of the time, Pallas kernels for 0%

commit v1 on v0

--- a/solution.py
+++ b/solution.py
@@ -41,7 +41,12 @@
     hidden = (jax.nn.silu(gate_act) * up_act).astype(jnp.bfloat16)
     columns = lax.all_to_all(weight_out, "tensor", split_axis=1, concat_axis=0, tiled=True)
     unit_count = hidden.shape[1]
-    shard_piece = lax.all_gather(hidden, "tensor", axis=1, tiled=True)
+    register_the_sheet = lambda mine: jnp.roll(
+        jnp.concatenate([mine, lax.ppermute(mine, "tensor", [(0, 1), (1, 0)])], axis=1),
+        lax.axis_index("tensor") * mine.shape[1],
+        1,
+    )
+    shard_piece = register_the_sheet(hidden)
     groups = shard_piece.shape[1] // unit_count
     weight_rows = columns
     weight_rows = weight_rows.reshape(groups, unit_count, columns.shape[1])

time: 213 us -> 214 us (level)
  blocking collectives: 41.5 us -> 4.69 us
  waiting for transfers between devices: 111 us -> 146 us
    all_gather x1 -> x0, blocking collectives: 36.8 us -> none  [body(): shard_piece = lax.all_gather(hidden, 'tensor', axis=1, tiled=True)]
    ppermute x0 -> x1, waiting for transfers between devices: none -> 35.3 us  [body(): lax.ppermute(mine, 'tensor', [(0, 1), (1, 0)])]
  transfers between devices with their start and end apart: 3 -> 4, of which waited for: 2 -> 3; matrix products, arithmetic and copies ran while one was open for 9% -> 10% of each run, Pallas kernels for 0% -> 0%
where the time goes in v1:
time: 214 us; the launch traced here: 213 us
  waiting for transfers between devices  146 us (68%)
  starting transfers between devices  19.9 us (9%)
  local copies, waits for them, and re-layouts  18.5 us (9%)
  matrix products  13.3 us (6%)
  other arithmetic  10.5 us (5%)
  blocking collectives  4.69 us (2%)
    all_to_all x1, waiting for transfers between devices, body(): lax.all_to_all(jnp.repeat(packed, 2, axis=0), 'expert', split_axis=0, con...  69.4 us
    all_to_all x1, waiting for transfers between devices, body(): lax.all_to_all(half_out.reshape(devices_wide, capacity, -1), 'expert', sp...  41.6 us
    ppermute x1, waiting for transfers between devices, body(): lax.ppermute(mine, 'tensor', [(0, 1), (1, 0)])  35.3 us
    dot_general x2, matrix products, rows_times(): lax.dot_general(rows, weight, (((1,), (1,)), ((), ())), preferred_element...  7.63 us
    all_to_all x1, starting transfers between devices, body(): lax.all_to_all(jnp.repeat(packed, 2, axis=0), 'expert', split_axis=0, con...  7.38 us
    unnamed x10, local copies, waits for them, and re-layouts  6.01 us
    all_to_all x1, local copies, waits for them, and re-layouts, body(): lax.all_to_all(weight_out, 'tensor', split_axis=1, concat_axis=0, tiled=T...  5.93 us
    all_to_all x1, starting transfers between devices, body(): lax.all_to_all(half_out.reshape(devices_wide, capacity, -1), 'expert', sp...  5.63 us
  transfers between devices with their start and end apart: 4, of which 3 were waited for; matrix products, arithmetic and copies ran while one was open for 10% of the time, Pallas kernels for 0%

profile of v1, /device:TPU:11, one launch (start us, length us, event | category | flops | bytes accessed | tf_op | source)
XLA Modules:
  0.0 213.3 jit_solution(10345774350778679764)
XLA Ops:
  0.0 0.7 convert_reduce_fusion
  0.7 0.7 bitcast_or_fusion
  1.4 0.1 copy.23
  1.5 0.1 copy.25
  1.6 0.1 reshape.55
  1.7 0.0 copy-start.1
  1.7 0.0 copy-start
  1.7 1.3 gather_fusion.1
  3.0 0.1 reshape.58
  3.1 0.1 copy.26
  3.1 0.0 copy-done.1
  3.2 0.1 copy.27
  3.2 0.1 fusion.15
  3.3 0.0 copy-done
  3.3 4.7 %all_gather.3 = bf16[16,7168]{1,0:T(8,128)(2,1)S(1)} all-gather(bf16[16,3584]{1,0:T(8,128)(2,1)S(1)} %copy-done), channel_id=1, replica_groups=mesh['expert'=16,'tensor'=2] {'tensor'}, dimensions={1}, use_global_device_ids=true | all-gather | bytes 344064 | tf_op jit(solution)/shard_map/all_gather | solution.py:33
  8.0 0.7 convolution_convert_fusion
  8.7 2.3 %broadcast_in_dim.16 = bf16[8,2,16,7168]{3,2,1,0:T(8,128)(2,1)} broadcast(bf16[8,16,7168]{2,1,0:T(8,128)(2,1)S(1)} %bitcast.39), dimensions={0,2,3} | broadcast | bytes 5505024 | tf_op jit(solution)/shard_map/broadcast_in_dim | solution.py:37
  11.0 7.4 %all-to-all-start = ((bf16[16,16,7168]{2,1,0:T(8,128)(2,1)}), bf16[16,16,7168]{2,1,0:T(8,128)(2,1)}, u32[]{:S(2)}, u32[]{:S(2)}) async-start(bf16[16,16,7168]{2,1,0:T(8,128)(2,1)} %bitcast.37), calls=%async_computation | async-start | bytes 7340032 | tf_op jit(solution)/shard_map/all_to_all | solution.py:36
  18.4 5.9 %copy.28 = bf16[1,256,7168]{1,2,0:T(8,128)(2,1)} copy(bf16[1,256,7168]{2,1,0:T(8,128)(2,1)} %param.11) | data formatting | bytes 7340032 | tf_op args[5]
  24.3 5.9 %copy.29 = bf16[256,2,3584]{2,0,1:T(8,128)(2,1)} copy(bf16[256,2,3584]{0,2,1:T(8,128)(2,1)} %bitcast.36) | data formatting | bytes 7340032 | tf_op jit(solution)/shard_map/all_to_all | solution.py:42
  30.2 69.4 %all-to-all-done = bf16[16,16,7168]{2,1,0:T(8,128)(2,1)} async-done(((bf16[16,16,7168]{2,1,0:T(8,128)(2,1)}), bf16[16,16,7168]{2,1,0:T(8,128)(2,1)}, u32[]{:S(2)}, u32[]{:S(2)}) %all-to-all-start) | async-done | bytes 3670048 | tf_op jit(solution)/shard_map/all_to_all | solution.py:36
  99.6 5.4 %all-to-all-start.1 = ((bf16[256,2,3584]{2,0,1:T(8,128)(2,1)}), bf16[256,2,3584]{2,0,1:T(8,128)(2,1)}, u32[]{:S(2)}, u32[]{:S(2)}) async-start(bf16[256,2,3584]{2,0,1:T(8,128)(2,1)} %copy.29), calls=%async_computation.1 | async-start | bytes 7340032 | tf_op jit(solution)/shard_map/all_to_all | solution.py:42
  105.0 0.0 copy-start.3
  105.0 4.4 %fusion.3 = f32[256,256]{0,1:T(8,128)S(1)} fusion(bf16[256,7168]{1,0:T(8,128)(2,1)} %bitcast.3, bf16[1,256,7168]{2,1,0:T(8,128)(2,1)} %param.9), kind=kOutput, calls=%fused_computation.7 | convolution fusion | flops 939524096 | bytes 7602176 | tf_op jit(solution)/shard_map/dot_general | solution.py:8
  109.5 0.0 copy-done.3
  109.5 3.2 %fusion.9 = bf16[256,256]{0,1:T(8,128)(2,1)S(1)} fusion(bf16[256,7168]{1,0:T(8,128)(2,1)} %bitcast.3, bf16[1,256,7168]{2,1,0:T(8,128)(2,1)S(1)} %copy-done.3, f32[256,256]{0,1:T(8,128)S(1)} %fusion.3), kind=kOutput, calls=%fused_computation.13 | convolution fusion | flops 939917312 | bytes 7733248 | tf_op jit(solution)/shard_map/dot_general | solution.py:8
  112.7 1.5 collective-permute-start
  114.2 35.3 %collective-permute-done = bf16[256,256]{0,1:T(8,128)(2,1)S(1)} collective-permute-done((bf16[256,256]{0,1:T(8,128)(2,1)S(1)}, bf16[256,256]{0,1:T(8,128)(2,1)S(1)}, u32[]{:S(2)}, u32[]{:S(2)}) %collective-permute-start) | collective-permute-done | bytes 131104 | tf_op jit(solution)/shard_map/ppermute | solution.py:45
  149.5 1.2 fusion.14
  150.7 0.0 all-to-all-done.1
  150.7 5.0 %convolution_convert_fusion.1 = bf16[2,256,3584]{2,1,0:T(8,128)(2,1)} fusion(bf16[256,2,256]{0,2,1:T(8,128)(2,1)S(1)} %bitcast.40, bf16[256,2,3584]{2,0,1:T(8,128)(2,1)} %all-to-all-done.1), kind=kOutput, calls=%fused_computation.3 | convolution fusion | flops 941359104 | bytes 7602176 | tf_op jit(solution)/shard_map/rgf,gfd->grd/dot_general | solution.py:54
  155.7 0.0 copy-start.2
  155.7 4.4 %reduce_sum.31 = bf16[256,3584]{1,0:T(8,128)(2,1)} reduce(bf16[2,256,3584]{2,1,0:T(8,128)(2,1)} %convolution_convert_fusion.1, bf16[]{:T(256)} %constant.58.clone.1), dimensions={0}, to_apply=%region_3.4 | reduce | flops 917504 | bytes 5505026 | tf_op jit(solution)/shard_map/reduce_sum | solution.py:58
  160.1 5.6 %all-to-all-start.2 = ((bf16[16,16,3584]{2,1,0:T(8,128)(2,1)}), bf16[16,16,3584]{2,1,0:T(8,128)(2,1)S(1)}, u32[]{:S(2)}, u32[]{:S(2)}) async-start(bf16[16,16,3584]{2,1,0:T(8,128)(2,1)} %bitcast.9), calls=%async_computation.2 | async-start | bytes 3670016 | tf_op jit(solution)/shard_map/all_to_all | solution.py:59
  165.7 0.1 copy.31
  165.8 0.1 reshape.49
  165.9 0.0 copy-done.2
  165.9 0.1 copy.22
  166.0 41.6 %all-to-all-done.2 = bf16[16,16,3584]{2,1,0:T(8,128)(2,1)S(1)} async-done(((bf16[16,16,3584]{2,1,0:T(8,128)(2,1)}), bf16[16,16,3584]{2,1,0:T(8,128)(2,1)S(1)}, u32[]{:S(2)}, u32[]{:S(2)}) %all-to-all-start.2) | async-done | bytes 1835040 | tf_op jit(solution)/shard_map/all_to_all | solution.py:59
  207.5 0.4 convert.2
  207.9 0.2 slice_add_fusion
  208.2 2.4 %gather_fusion = f32[128,3584]{1,0:T(8,128)} fusion(f32[128,3584]{1,0:T(8,128)S(1)} %bitcast.35, s32[1024]{0:T(1024)S(1)} %pad_clamp_fusion), kind=kCustom, calls=%fused_computation | custom fusion | bytes 3670528 | tf_op jit(solution)/shard_map/gather | solution.py:68
  210.6 2.8 %fusion.5 = bf16[16,3584]{1,0:T(8,128)(2,1)} fusion(f32[128,3584]{1,0:T(8,128)} %gather_fusion, f32[16,8]{1,0:T(8,128)S(1)} %copy.22), kind=kLoop, calls=%fused_computation.11 | loop fusion | flops 860160 | bytes 1950208 | tf_op jit(solution)/shard_map/reduce_sum | solution.py:69
  (4 shorter events, 0.1 us)
Async XLA Ops:
  1.7 1.5 copy-start.1
  1.7 1.6 copy-start
  11.0 88.6 %all-to-all-start = ((bf16[16,16,7168]{2,1,0:T(8,128)(2,1)}), bf16[16,16,7168]{2,1,0:T(8,128)(2,1)}, u32[]{:S(2)}, u32[]{:S(2)}) async-start(bf16[16,16,7168]{2,1,0:T(8,128)(2,1)} %bitcast.37), calls=%async_computation | async-start | bytes 7340032 | tf_op jit(solution)/shard_map/all_to_all | solution.py:36
  99.6 51.1 %all-to-all-start.1 = ((bf16[256,2,3584]{2,0,1:T(8,128)(2,1)}), bf16[256,2,3584]{2,0,1:T(8,128)(2,1)}, u32[]{:S(2)}, u32[]{:S(2)}) async-start(bf16[256,2,3584]{2,0,1:T(8,128)(2,1)} %copy.29), calls=%async_computation.1 | async-start | bytes 7340032 | tf_op jit(solution)/shard_map/all_to_all | solution.py:42
  105.0 4.5 %copy-start.3 = (bf16[1,256,7168]{2,1,0:T(8,128)(2,1)S(1)}, bf16[1,256,7168]{2,1,0:T(8,128)(2,1)}, u32[]{:S(2)}) copy-start(bf16[1,256,7168]{2,1,0:T(8,128)(2,1)} %param.10) | copy-start | bytes 11010052
  112.7 36.8 %collective-permute-start = (bf16[256,256]{0,1:T(8,128)(2,1)S(1)}, bf16[256,256]{0,1:T(8,128)(2,1)S(1)}, u32[]{:S(2)}, u32[]{:S(2)}) collective-permute-start(bf16[256,256]{0,1:T(8,128)(2,1)S(1)} %fusion.9), channel_id=1, source_target_pairs={{0,1},{1,0},{2,3},{3,2},{4,5},{5,4},{6,7},{7,6},{8,9},{9,8},{10,11... | collective-permute-start | bytes 393224 | tf_op jit(solution)/shard_map/ppermute | solution.py:45
  155.7 10.2 %copy-start.2 = (f32[16,8]{0,1:T(8,128)S(1)}, f32[16,8]{0,1:T(8,128)}, u32[]{:S(2)}) copy-start(f32[16,8]{0,1:T(8,128)} %param.8) | copy-start | bytes 1540
  160.1 47.4 %all-to-all-start.2 = ((bf16[16,16,3584]{2,1,0:T(8,128)(2,1)}), bf16[16,16,3584]{2,1,0:T(8,128)(2,1)S(1)}, u32[]{:S(2)}, u32[]{:S(2)}) async-start(bf16[16,16,3584]{2,1,0:T(8,128)(2,1)} %bitcast.9), calls=%async_computation.2 | async-start | bytes 3670016 | tf_op jit(solution)/shard_map/all_to_all | solution.py:59
